TPU v7x, 32 devices: a whole 2x2x4 slice. The times are simulated.
32 devices in a mesh: group: 2 (over y), visit: 16 (over z, x, core), sky: 1.
Axes of the slice: x: 2, y: 2, z: 4, core: 2. Of those that a mesh axis runs over, the one named last changes fastest.
Arguments:
- template: bfloat16 [64, 128], P(('group', 'visit'), 'sky'), parts along dimension 0, may hold values from -6 to 6
- science: float32 [32, 32, 128], P(('group', 'visit'), None, 'sky'), parts along dimension 0, may hold values from -15 to 15
- variance: float32 [32, 32, 128], P(('group', 'visit'), None, 'sky'), parts along dimension 0, may hold values from 0.5 to 4
- col_taps: bfloat16 [49, 31], replicated, may hold values from -1 to 1
- row_taps: bfloat16 [49, 31], replicated, may hold values from -1 to 1
- stamp_rows: int32 [32, 1, 16], P(('group', 'visit'), 'sky'), parts along dimension 0, may hold values from 0 to 16
- stamp_cols: int32 [32, 1, 16], P(('group', 'visit'), 'sky'), parts along dimension 0, may hold values from 0 to 112
Outputs:
- difference: float32 [32, 32, 128], P(('group', 'visit'), None, 'sky'), parts along dimension 0
- coefficients: float32 [32, 50], P(('group', 'visit')), parts along dimension 0
- detection: float32 [64, 128], P(('group', 'visit'), 'sky'), parts along dimension 0
There are 2 independent parts, one for each index of `group`. A program takes and returns all parts, laid end to end along the dimension named above; an argument that names none is the same for every part. Nothing has to cross between parts.
All inputs are finite; a program needn't handle non-finite values.
Results may differ from a plain program's by a relative error of at most 0.0018.
Values may be sent and summed in bfloat16 or wider, within the bound.
No kernel may reach another device: no remote copies, remote signals or barrier semaphores. Data moves between devices by JAX's collectives and lax.ppermute only.
A program may use at most 128 MiB of HBM per device.

v0:
```python
import jax
import jax.numpy as jnp
from jax import lax
from jax.sharding import PartitionSpec as P

KBLK = 7
STAMP = 16


def with_halo(cells, sides, width):
    for axis, dim in sides:
        count = lax.axis_size(axis)
        ends = count - 1
        head = lax.slice_in_dim(cells, 0, width, axis=dim)
        tail = lax.slice_in_dim(cells, cells.shape[dim] - width, cells.shape[dim], axis=dim)
        cells = jnp.concatenate(
            [
                lax.ppermute(tail, axis, [(i, (i + 1) % count) for i in range(ends)]),
                cells,
                lax.ppermute(head, axis, [((i + 1) % count, i) for i in range(ends)]),
            ],
            axis=dim,
        )
    return cells


def tap_selectors(out_len, in_len, tap_count):
    offsets = (
        jnp.arange(in_len, dtype=jnp.int32)[None, :] - jnp.arange(out_len, dtype=jnp.int32)[:, None]
    )
    return (offsets[None, :, :] == jnp.arange(tap_count, dtype=jnp.int32)[:, None, None]).astype(
        jnp.float32
    )


def column_pass(padded, taps_block):
    tap_count = taps_block.shape[1]
    out_width = padded.shape[1] - tap_count + 1
    selectors = tap_selectors(out_width, padded.shape[1], tap_count)
    band_mats = jnp.einsum("kj,jci->kic", taps_block.astype(jnp.float32), selectors).astype(
        jnp.bfloat16
    )
    result = jnp.einsum("ri,kic->krc", padded, band_mats, preferred_element_type=jnp.float32)
    return result.astype(jnp.bfloat16)


def band_matrix(taps_block, out_len, in_len):
    tap_count = taps_block.shape[1]
    offsets = (
        jnp.arange(in_len, dtype=jnp.int32)[None, :] - jnp.arange(out_len, dtype=jnp.int32)[:, None]
    )
    taps_wide = taps_block.astype(jnp.float32)
    band = jnp.zeros((taps_block.shape[0], out_len, in_len), jnp.float32)
    for offset in range(tap_count):
        band = band + jnp.where(
            offsets[None, :, :] == offset, taps_wide[:, offset][:, None, None], 0.0
        )
    return band.astype(jnp.bfloat16)


def row_pass(columns, taps_block):
    tap_count = taps_block.shape[1]
    margin = (tap_count - 1) // 2
    height = columns.shape[1]
    stride = min(512, height)
    padded = jnp.pad(columns, ((0, 0), (margin, margin), (0, 0)))
    band = band_matrix(taps_block, stride, stride + 2 * margin)
    pieces = jnp.einsum("kti,kiw->ktw", band, padded, preferred_element_type=jnp.float32).astype(
        jnp.bfloat16
    )
    return pieces


def extract_stamps(block, row_starts, col_starts):

    def extract(row_start, col_start):
        return lax.dynamic_slice(
            block, (jnp.int32(0), row_start, col_start), (block.shape[0], STAMP, STAMP)
        )

    stamps = jax.vmap(extract)(row_starts, col_starts)
    return jnp.transpose(stamps, (1, 0, 2, 3)).reshape(block.shape[0], -1)


def extract_plane(plane, row_starts, col_starts):

    def extract(row_start, col_start):
        return lax.dynamic_slice(plane, (row_start, col_start), (STAMP, STAMP))

    return jax.vmap(extract)(row_starts, col_starts).reshape(-1)


def cholesky_solve(matrix, vector):
    factor = jnp.linalg.cholesky(matrix)
    middle = lax.linalg.triangular_solve(factor, vector[:, None], left_side=True, lower=True)
    answer = lax.linalg.triangular_solve(
        factor, middle, left_side=True, lower=True, transpose_a=True
    )
    return answer[:, 0]


def on_device(template, science, variance, col_taps, row_taps, stamp_rows, stamp_cols):
    tap_count = col_taps.shape[1]
    margin = (tap_count - 1) // 2
    kernels = col_taps.shape[0]
    blocks = kernels // KBLK
    science_map = science[0]
    variance_map = variance[0]
    inverse = 1.0 / variance_map
    gathered = lax.all_gather(template, "visit", axis=0, tiled=True)
    padded_tile = with_halo(gathered, (("sky", 1),), margin)
    image_list = []
    for block_index in range(blocks):
        image_list.append(
            row_pass(
                column_pass(padded_tile, col_taps[block_index * KBLK : (block_index + 1) * KBLK]),
                row_taps[block_index * KBLK : (block_index + 1) * KBLK],
            )
        )
    convolved = jnp.concatenate(image_list, axis=0)
    row_starts = stamp_rows[0, 0]
    col_starts = stamp_cols[0, 0]
    design_core = extract_stamps(convolved, row_starts, col_starts)
    design = jnp.concatenate(
        [design_core, jnp.ones((1, design_core.shape[1]), design_core.dtype)], axis=0
    ).astype(jnp.float32)
    weights = 1.0 / extract_plane(variance_map, row_starts, col_starts)
    values = extract_plane(science_map, row_starts, col_starts)
    partial_normal = jnp.dot(design * weights[None, :], design.T, precision=lax.Precision.HIGHEST)
    partial_target = jnp.dot(design, weights * values, precision=lax.Precision.HIGHEST)
    normal, target = lax.psum((partial_normal, partial_target), "sky")
    solution = cholesky_solve(normal, target)

    def model_step(block_index, total):
        images = lax.dynamic_slice_in_dim(convolved, block_index * KBLK, KBLK, 0).astype(
            jnp.float32
        )
        share = lax.dynamic_slice_in_dim(solution, block_index * KBLK, KBLK, 0)
        return total + jnp.tensordot(share, images, axes=1, precision=lax.Precision.HIGHEST)

    model_map = lax.fori_loop(0, blocks, model_step, jnp.zeros(science_map.shape, jnp.float32))
    residual = science_map - model_map - solution[kernels]
    difference = (residual / jnp.sqrt(variance_map))[None, :, :]
    weighted = residual / variance_map
    numerator, weight_total = (
        lax.psum_scatter(weighted, "visit", scatter_dimension=0, tiled=True),
        lax.psum_scatter(inverse, "visit", scatter_dimension=0, tiled=True),
    )
    detection = numerator / jnp.sqrt(weight_total)
    return (difference, solution[None, :], detection)


def solution(mesh):
    in_specs = (
        P(("group", "visit"), "sky"),
        P(("group", "visit"), None, "sky"),
        P(("group", "visit"), None, "sky"),
        P(),
        P(),
        P(("group", "visit"), "sky", None),
        P(("group", "visit"), "sky", None),
    )
    out_specs = (
        P(("group", "visit"), None, "sky"),
        P(("group", "visit"), None),
        P(("group", "visit"), "sky"),
    )
    return jax.shard_map(
        on_device, mesh=mesh, in_specs=in_specs, out_specs=out_specs, check_vma=False
    )
```

profile of v0, /device:TPU:0, one launch (start us, length us, event | category | flops | bytes accessed | tf_op | source)
XLA Modules:
  0.0 237.8 jit_solution(4948356048800179354)
XLA Ops:
  0.6 23.3 %all-gather = bf16[16,2,128]{2,1,0:T(2,128)(2,1)S(1)} all-gather(bf16[1,2,128]{2,1,0:T(2,128)(2,1)} %bitcast.593), channel_id=1, replica_groups=mesh['group'=2,'visit'=16,'sky'=1] {'visit'}, dimensions={0}, use_global_device_ids=true | all-gather | bytes 8704 | tf_op jit(solution)/shard_map/all_gather | solution.py:110
  26.7 1.7 fusion.34
  28.4 1.8 fusion.33
  30.2 1.7 fusion.32
  32.0 1.8 fusion.31
  33.9 1.8 fusion.30
  35.7 1.8 fusion.29
  37.6 1.9 fusion.28
  39.5 30.6 %while.18 = (s32[]{:T(128)}, f32[32,128]{1,0:T(8,128)S(1)}, s32[16,2]{0,1:T(2,128)S(1)}, f32[16,16,16]{2,1,0:T(8,128)S(1)}, s32[]{:T(128)}) while((s32[]{:T(128)}, f32[32,128]{1,0:T(8,128)S(1)}, s32[16,2]{0,1:T(2,128)S(1)}, f32[16,16,16]{2,1,0:T(8,128)S(1)}, s32[]{:T(128)}) %tuple.319), condition=%wide.while_cond.1, body=%wide.while_body.1.sunk | while | flops 2 | bytes 16493 | solution.py:88
  70.1 31.5 %while.19 = (s32[]{:T(128)}, f32[32,128]{1,0:T(8,128)S(1)}, s32[16,2]{0,1:T(2,128)S(1)}, f32[16,16,16]{2,1,0:T(8,128)S(1)}, s32[]{:T(128)}) while((s32[]{:T(128)}, f32[32,128]{1,0:T(8,128)S(1)}, s32[16,2]{0,1:T(2,128)S(1)}, f32[16,16,16]{2,1,0:T(8,128)S(1)}, s32[]{:T(128)}) %tuple.321), condition=%wide.while_cond.2, body=%wide.while_body.2.sunk | while | flops 2 | bytes 16493 | solution.py:88
  70.7 1.4 bitcast_dynamic-update-slice_fusion.8
  72.7 1.4 bitcast_dynamic-update-slice_fusion.8
  74.7 1.4 bitcast_dynamic-update-slice_fusion.8
  76.6 1.4 bitcast_dynamic-update-slice_fusion.8
  78.6 1.4 bitcast_dynamic-update-slice_fusion.8
  80.6 1.4 bitcast_dynamic-update-slice_fusion.8
  82.5 1.4 bitcast_dynamic-update-slice_fusion.8
  84.5 1.4 bitcast_dynamic-update-slice_fusion.8
  86.5 1.4 bitcast_dynamic-update-slice_fusion.8
  88.4 1.4 bitcast_dynamic-update-slice_fusion.8
  90.4 1.4 bitcast_dynamic-update-slice_fusion.8
  92.4 1.4 bitcast_dynamic-update-slice_fusion.8
  94.3 1.4 bitcast_dynamic-update-slice_fusion.8
  96.3 1.4 bitcast_dynamic-update-slice_fusion.8
  98.3 1.4 bitcast_dynamic-update-slice_fusion.8
  112.6 45.1 %while.17 = (s32[]{:T(128)}, bf16[49,32,128]{2,1,0:T(8,128)(2,1)S(1)}, s32[16,3]{0,1:T(4,128)S(1)}, bf16[16,49,16,16]{3,2,1,0:T(8,128)(2,1)}, s32[]{:T(128)}) while((s32[]{:T(128)}, bf16[49,32,128]{2,1,0:T(8,128)(2,1)S(1)}, s32[16,3]{0,1:T(4,128)S(1)}, bf16[16,49,16,16]{3,2,1,0:T(8,128)(2,1)}, s32[]{:T(128)}) %tuple.312), condition=%wide.while_cond, body=%wide.while_body.sunk | while | flops 2 | bytes 227433 | solution.py:77
  113.3 2.1 bitcast_dynamic-update-slice_fusion.6
  116.1 2.1 bitcast_dynamic-update-slice_fusion.6
  118.9 2.2 bitcast_dynamic-update-slice_fusion.6
  121.8 2.2 bitcast_dynamic-update-slice_fusion.6
  124.6 2.1 bitcast_dynamic-update-slice_fusion.6
  127.4 2.2 bitcast_dynamic-update-slice_fusion.6
  130.2 2.1 bitcast_dynamic-update-slice_fusion.6
  133.0 2.2 bitcast_dynamic-update-slice_fusion.6
  135.9 2.1 bitcast_dynamic-update-slice_fusion.6
  138.7 2.2 bitcast_dynamic-update-slice_fusion.6
  141.5 2.2 bitcast_dynamic-update-slice_fusion.6
  144.3 2.2 bitcast_dynamic-update-slice_fusion.6
  147.1 2.2 bitcast_dynamic-update-slice_fusion.6
  150.0 2.1 bitcast_dynamic-update-slice_fusion.6
  152.8 2.2 bitcast_dynamic-update-slice_fusion.6
  155.6 2.1 bitcast_dynamic-update-slice_fusion.6
  157.7 4.3 %copy.27 = bf16[49,16,16,16]{0,3,2,1:T(8,128)(2,1)S(1)} copy(bf16[49,16,16,16]{3,2,0,1:T(8,128)(2,1)} %bitcast.581) | data formatting | bytes 802816 | tf_op jit(solution)/shard_map/transpose | solution.py:82
  162.1 2.4 %fusion.11 = f32[50,50]{1,0:T(8,128)S(1)} fusion(f32[4096]{0:T(1024)S(1)} %div.38, bf16[49,4096]{0,1:T(8,128)(2,1)S(1)} %bitcast.579), kind=kOutput, calls=%fused_computation.20 | convolution fusion | flops 123289600 | bytes 427792 | tf_op jit(solution)/shard_map/dot_general | solution.py:129
  164.6 4.6 %cholesky.16 = f32[50,50]{1,0:T(8,128)S(1)} custom-call(f32[50,50]{1,0:T(8,128)S(1)} %fusion.511), custom_call_target="Cholesky" | custom-call | tf_op jit(solution)/shard_map/jit(cholesky)/cholesky | solution.py:94
  170.5 3.8 %custom-call.8 = f32[1,50,50]{1,2,0:T(8,128)S(1)} custom-call(f32[1,50,50]{2,1,0:T(8,128)S(1)} %fusion.507), custom_call_target="InvertDiagBlocksLowerTriangular" | custom-call | tf_op jit(solution)/shard_map/triangular_solve | solution.py:96
  175.8 2.3 while.20
  179.5 57.8 %all-reduce.10 = (f32[32,128]{1,0:T(8,128)S(1)}, f32[32,128]{1,0:T(8,128)S(1)}) all-reduce(f32[32,128]{1,0:T(8,128)S(1)} %get-tuple-element.164, f32[32,128]{1,0:T(8,128)S(1)} %get-tuple-element.162), channel_id=3, replica_groups=mesh['group'=2,'visit'=16,'sky'=1] {'visit'}, use_global_device_ids=true, to_apply=%region_5.6.clone | all-reduce | flops 8192 | bytes 65536
  (226 shorter events, 71.5 us)
Async XLA Ops:
  0.6 31.4 %copy-start.5 = (bf16[49,31]{0,1:T(8,128)(2,1)S(1)}, bf16[49,31]{0,1:T(8,128)(2,1)}, u32[]{:S(2)}) copy-start(bf16[49,31]{0,1:T(8,128)(2,1)} %param.12) | copy-start | bytes 9118
  24.0 79.1 %collective-permute-start = (bf16[32,15]{1,0:T(8,128)(2,1)S(1)}, bf16[32,15]{1,0:T(8,128)(2,1)S(1)}, u32[]{:S(2)}, u32[]{:S(2)}) collective-permute-start(bf16[32,15]{1,0:T(8,128)(2,1)S(1)} %get-tuple-element.389), channel_id=1, source_target_pairs={} | collective-permute-start | bytes 2888 | tf_op jit(solution)/shard_map/ppermute | solution.py:18
  24.6 78.5 %collective-permute-start.1 = (bf16[32,15]{1,0:T(8,128)(2,1)S(1)}, bf16[32,15]{1,0:T(8,128)(2,1)S(1)}, u32[]{:S(2)}, u32[]{:S(2)}) collective-permute-start(bf16[32,15]{1,0:T(8,128)(2,1)S(1)} %get-tuple-element.390), channel_id=1, source_target_pairs={} | collective-permute-start | bytes 2888 | tf_op jit(solution)/shard_map/ppermute | solution.py:20
  28.4 11.0 %copy-start.3 = (s32[1,1,16]{2,1,0:T(1,128)S(1)}, s32[1,1,16]{2,1,0:T(1,128)}, u32[]{:S(2)}) copy-start(s32[1,1,16]{2,1,0:T(1,128)} %param.15) | copy-start | bytes 196
  28.4 11.0 %copy-start.4 = (s32[1,1,16]{2,1,0:T(1,128)S(1)}, s32[1,1,16]{2,1,0:T(1,128)}, u32[]{:S(2)}) copy-start(s32[1,1,16]{2,1,0:T(1,128)} %param.14) | copy-start | bytes 196
  30.2 9.3 %copy-start = (f32[1,32,128]{2,1,0:T(8,128)S(1)}, f32[1,32,128]{2,1,0:T(8,128)}, u32[]{:S(2)}) copy-start(f32[1,32,128]{2,1,0:T(8,128)} %param.11) | copy-start | bytes 49156
  30.2 39.9 %copy-start.1 = (f32[1,32,128]{2,1,0:T(8,128)S(1)}, f32[1,32,128]{2,1,0:T(8,128)}, u32[]{:S(2)}) copy-start(f32[1,32,128]{2,1,0:T(8,128)} %param.10) | copy-start | bytes 49156
  32.0 69.9 %copy-start.6 = (u32[32]{0:T(128)S(1)}, u32[32]{0:T(128)}, u32[]{:S(2)}) copy-start(u32[32]{0:T(128)} %constant.223) | copy-start | bytes 388
  103.1 4.8 %copy-start.7 = (bf16[7,158,128]{1,0,2:T(8,128)(2,1)S(1)}, bf16[7,158,128]{1,0,2:T(8,128)(2,1)}, u32[]{:S(2)}) copy-start(bf16[7,158,128]{1,0,2:T(8,128)(2,1)} %fusion.28) | copy-start | bytes 849412
  178.2 59.7 %copy-start.2 = (f32[50]{0:T(128)}, f32[50]{0:T(128)S(1)}, u32[]{:S(2)}) copy-start(f32[50]{0:T(128)S(1)} %get-tuple-element.611) | copy-start | bytes 604
where the time goes:
time: 239 us; the launch traced here: 238 us
  local copies, waits for them, and re-layouts  113 us (47%)
  blocking collectives  81.1 us (34%)
  matrix products  27 us (11%)
  other arithmetic  13 us (5%)
    gather x144, local copies, waits for them, and re-layouts  107 us
    unnamed x1, blocking collectives  57.8 us
    all_gather x1, blocking collectives, on_device(): gathered = lax.all_gather(template, 'visit', axis=0, tiled=True)  23.3 us
    dot_general x7, matrix products, column_pass(): jnp.einsum('kj,jci->kic', taps_block.astype(jnp.float32), selectors)  12.6 us
    another operation x3, other arithmetic, cholesky_solve(): factor = jnp.linalg.cholesky(matrix)  5.24 us
    dot_general x7, matrix products, column_pass(): jnp.einsum('ri,kic->krc', padded, band_mats, preferred_element_type=jnp.f...  4.89 us
  transfers between devices with their start and end apart: 2, of which 0 were waited for; matrix products, arithmetic and copies ran while one was open for 32% of the time, Pallas kernels for 0%

commit v1 on v0

--- a/solution.py
+++ b/solution.py
@@ -107,7 +107,15 @@
     science_map = science[0]
     variance_map = variance[0]
     inverse = 1.0 / variance_map
-    gathered = lax.all_gather(template, "visit", axis=0, tiled=True)
+    ways, here = (lax.axis_size("visit"), lax.axis_index("visit"))
+    grown, reach = (template, 1)
+    while reach < ways:
+        theirs = lax.ppermute(grown, "visit", [(d, d ^ reach) for d in range(ways)])
+        mine_first = jnp.concatenate([grown, theirs], axis=0)
+        theirs_first = jnp.concatenate([theirs, grown], axis=0)
+        grown = jnp.where(here & reach == 0, mine_first, theirs_first)
+        reach = 2 * reach
+    gathered = grown
     padded_tile = with_halo(gathered, (("sky", 1),), margin)
     image_list = []
     for block_index in range(blocks):

time: 239 us -> 229 us (0.958)
  blocking collectives: 81.1 us -> 59 us
  starting transfers between devices: 1.3 us -> 9.8 us
  waiting for transfers between devices: 0.01 us -> 4.67 us
    all_gather x1 -> x0, blocking collectives: 23.3 us -> none  [on_device(): gathered = lax.all_gather(template, 'visit', axis=0, tiled=True)]
    ppermute x0 -> x4, starting transfers between devices: none -> 8.32 us  [on_device(): theirs = lax.ppermute(grown, 'visit', [(d, d ^ reach) for d in range(ways)])]
    ppermute x0 -> x4, waiting for transfers between devices: none -> 4.66 us  [on_device(): theirs = lax.ppermute(grown, 'visit', [(d, d ^ reach) for d in range(ways)])]
  transfers between devices with their start and end apart: 2 -> 6, of which waited for: 0 -> 3; matrix products, arithmetic and copies ran while one was open for 32% -> 34% of each run, Pallas kernels for 0% -> 0%
where the time goes in v1:
time: 229 us; the launch traced here: 227 us
  local copies, waits for them, and re-layouts  112 us (49%)
  blocking collectives  59 us (26%)
  matrix products  27 us (12%)
  other arithmetic  13 us (6%)
  starting transfers between devices  9.8 us (4%)
  waiting for transfers between devices  4.67 us (2%)
    gather x144, local copies, waits for them, and re-layouts  106 us
    unnamed x1, blocking collectives  59 us
    dot_general x7, matrix products, column_pass(): jnp.einsum('kj,jci->kic', taps_block.astype(jnp.float32), selectors)  12.5 us
    ppermute x4, starting transfers between devices, on_device(): theirs = lax.ppermute(grown, 'visit', [(d, d ^ reach) for d in range(ways)])  8.32 us
    another operation x3, other arithmetic, cholesky_solve(): factor = jnp.linalg.cholesky(matrix)  5.24 us
    dot_general x7, matrix products, column_pass(): jnp.einsum('ri,kic->krc', padded, band_mats, preferred_element_type=jnp.f...  4.89 us
    ppermute x4, waiting for transfers between devices, on_device(): theirs = lax.ppermute(grown, 'visit', [(d, d ^ reach) for d in range(ways)])  4.66 us
  transfers between devices with their start and end apart: 6, of which 3 were waited for; matrix products, arithmetic and copies ran while one was open for 34% of the time, Pallas kernels for 0%

profile of v1, /device:TPU:0, one launch (start us, length us, event | category | flops | bytes accessed | tf_op | source)
XLA Modules:
  0.0 227.5 jit_solution(17007917748574673735)
XLA Ops:
  2.5 1.7 fusion.34
  4.2 1.8 fusion.33
  6.0 1.7 fusion.32
  7.8 1.8 fusion.31
  9.7 1.8 fusion.30
  11.5 1.8 fusion.29
  13.4 1.9 fusion.28
  15.4 32.2 %while.18 = (s32[]{:T(128)}, f32[32,128]{1,0:T(8,128)S(1)}, s32[16,2]{0,1:T(2,128)S(1)}, f32[16,16,16]{2,1,0:T(8,128)S(1)}, s32[]{:T(128)}) while((s32[]{:T(128)}, f32[32,128]{1,0:T(8,128)S(1)}, s32[16,2]{0,1:T(2,128)S(1)}, f32[16,16,16]{2,1,0:T(8,128)S(1)}, s32[]{:T(128)}) %tuple.319), condition=%wide.while_cond.1, body=%wide.while_body.1.sunk | while | flops 2 | bytes 16493 | solution.py:88
  47.6 31.5 %while.19 = (s32[]{:T(128)}, f32[32,128]{1,0:T(8,128)S(1)}, s32[16,2]{0,1:T(2,128)S(1)}, f32[16,16,16]{2,1,0:T(8,128)S(1)}, s32[]{:T(128)}) while((s32[]{:T(128)}, f32[32,128]{1,0:T(8,128)S(1)}, s32[16,2]{0,1:T(2,128)S(1)}, f32[16,16,16]{2,1,0:T(8,128)S(1)}, s32[]{:T(128)}) %tuple.321), condition=%wide.while_cond.2, body=%wide.while_body.2.sunk | while | flops 2 | bytes 16493 | solution.py:88
  48.2 1.4 bitcast_dynamic-update-slice_fusion.8
  50.1 1.4 bitcast_dynamic-update-slice_fusion.8
  52.1 1.4 bitcast_dynamic-update-slice_fusion.8
  54.1 1.4 bitcast_dynamic-update-slice_fusion.8
  56.0 1.4 bitcast_dynamic-update-slice_fusion.8
  58.0 1.4 bitcast_dynamic-update-slice_fusion.8
  61.9 1.4 bitcast_dynamic-update-slice_fusion.8
  65.9 1.4 bitcast_dynamic-update-slice_fusion.8
  69.8 1.4 bitcast_dynamic-update-slice_fusion.8
  73.7 1.4 bitcast_dynamic-update-slice_fusion.8
  79.1 2.6 %collective-permute-start.1 = (bf16[4,128]{1,0:T(4,128)(2,1)S(1)}, bf16[4,128]{1,0:T(4,128)(2,1)S(1)}, u32[]{:S(2)}, u32[]{:S(2)}) collective-permute-start(bf16[4,128]{1,0:T(4,128)(2,1)S(1)} %maximum_select_fusion.3), channel_id=1, source_target_pairs={{0,2},{1,3},{2,0},{3,1},{4,6},{5,7},{6,4},{7,5},{8,10},{9,11},{10,... | collective-permute-start | bytes 3080 | tf_op jit(solution)/shard_map/ppermute | solution.py:113
  81.7 1.5 collective-permute-done.1
  83.2 2.2 collective-permute-start.2
  85.4 1.6 collective-permute-done.2
  87.0 3.0 %collective-permute-start.3 = (bf16[16,128]{1,0:T(8,128)(2,1)S(1)}, bf16[16,128]{1,0:T(8,128)(2,1)S(1)}, u32[]{:S(2)}, u32[]{:S(2)}) collective-permute-start(bf16[16,128]{1,0:T(8,128)(2,1)S(1)} %maximum_select_fusion.1), channel_id=1, source_target_pairs={{0,8},{1,9},{2,10},{3,11},{4,12},{5,13},{6,14},{7,15},{8,0},{9,1},... | collective-permute-start | bytes 12296 | tf_op jit(solution)/shard_map/ppermute | solution.py:113
  90.0 1.6 collective-permute-done.3
  104.2 42.0 %while.17 = (s32[]{:T(128)}, bf16[49,32,128]{2,1,0:T(8,128)(2,1)S(1)}, s32[16,3]{0,1:T(4,128)S(1)}, bf16[16,49,16,16]{3,2,1,0:T(8,128)(2,1)}, s32[]{:T(128)}) while((s32[]{:T(128)}, bf16[49,32,128]{2,1,0:T(8,128)(2,1)S(1)}, s32[16,3]{0,1:T(4,128)S(1)}, bf16[16,49,16,16]{3,2,1,0:T(8,128)(2,1)}, s32[]{:T(128)}) %tuple.312), condition=%wide.while_cond, body=%wide.while_body.sunk | while | flops 2 | bytes 227433 | solution.py:77
  104.8 2.0 bitcast_dynamic-update-slice_fusion.6
  107.4 2.0 bitcast_dynamic-update-slice_fusion.6
  110.0 2.0 bitcast_dynamic-update-slice_fusion.6
  112.6 2.1 bitcast_dynamic-update-slice_fusion.6
  115.3 2.0 bitcast_dynamic-update-slice_fusion.6
  117.9 2.0 bitcast_dynamic-update-slice_fusion.6
  120.6 2.0 bitcast_dynamic-update-slice_fusion.6
  123.2 2.0 bitcast_dynamic-update-slice_fusion.6
  125.8 2.0 bitcast_dynamic-update-slice_fusion.6
  128.4 2.0 bitcast_dynamic-update-slice_fusion.6
  131.0 2.0 bitcast_dynamic-update-slice_fusion.6
  133.7 2.0 bitcast_dynamic-update-slice_fusion.6
  136.3 2.0 bitcast_dynamic-update-slice_fusion.6
  138.9 2.0 bitcast_dynamic-update-slice_fusion.6
  141.5 2.0 bitcast_dynamic-update-slice_fusion.6
  144.2 2.0 bitcast_dynamic-update-slice_fusion.6
  146.2 4.3 %copy.27 = bf16[49,16,16,16]{0,3,2,1:T(8,128)(2,1)S(1)} copy(bf16[49,16,16,16]{3,2,0,1:T(8,128)(2,1)} %bitcast.579) | data formatting | bytes 802816 | tf_op jit(solution)/shard_map/transpose | solution.py:82
  150.5 2.4 %fusion.11 = f32[50,50]{1,0:T(8,128)S(1)} fusion(f32[4096]{0:T(1024)S(1)} %div.38, bf16[49,4096]{0,1:T(8,128)(2,1)S(1)} %bitcast.577), kind=kOutput, calls=%fused_computation.20 | convolution fusion | flops 123289600 | bytes 427792 | tf_op jit(solution)/shard_map/dot_general | solution.py:137
  153.1 4.6 %cholesky.16 = f32[50,50]{1,0:T(8,128)S(1)} custom-call(f32[50,50]{1,0:T(8,128)S(1)} %fusion.511), custom_call_target="Cholesky" | custom-call | tf_op jit(solution)/shard_map/jit(cholesky)/cholesky | solution.py:94
  159.0 3.8 %custom-call.8 = f32[1,50,50]{1,2,0:T(8,128)S(1)} custom-call(f32[1,50,50]{2,1,0:T(8,128)S(1)} %fusion.507), custom_call_target="InvertDiagBlocksLowerTriangular" | custom-call | tf_op jit(solution)/shard_map/triangular_solve | solution.py:96
  164.3 2.3 %while.20 = (s32[]{:T(128)}, f32[32,128]{1,0:T(8,128)S(1)}, f32[50]{0:T(128)S(1)}, bf16[49,32,128]{2,1,0:T(8,128)(2,1)S(1)}, s32[]{:T(128)}, /*index=5*/s32[]{:T(128)}, s32[]{:T(128)}, s32[]{:T(128)}, s32[]{:T(128)}) while((s32[]{:T(128)}, f32[32,128]{1,0:T(8,128)S(1)}, f32[50]{0:T(128)S(1)}, bf16[49,32,128]{2,1,0:T(8,128)(2,1)S(1)}, ...), condition=%wide.region_3.4_spmd.clone, body=%wide.region_2.3_spmd.clone.sunk | while | flops 352265 | bytes 237950 | solution.py:149
  167.9 59.0 %all-reduce.10 = (f32[32,128]{1,0:T(8,128)S(1)}, f32[32,128]{1,0:T(8,128)S(1)}) all-reduce(f32[32,128]{1,0:T(8,128)S(1)} %get-tuple-element.164, f32[32,128]{1,0:T(8,128)S(1)} %get-tuple-element.162), channel_id=3, replica_groups=mesh['group'=2,'visit'=16,'sky'=1] {'visit'}, use_global_device_ids=true, to_apply=%region_5.6.clone | all-reduce | flops 8192 | bytes 65536
  (239 shorter events, 79.8 us)
Async XLA Ops:
  0.6 7.2 %copy-start.6 = (bf16[49,31]{0,1:T(8,128)(2,1)S(1)}, bf16[49,31]{0,1:T(8,128)(2,1)}, u32[]{:S(2)}) copy-start(bf16[49,31]{0,1:T(8,128)(2,1)} %param.12) | copy-start | bytes 9118
  0.6 78.4 %collective-permute-start = (bf16[2,128]{1,0:T(2,128)(2,1)}, bf16[2,128]{1,0:T(2,128)(2,1)S(1)}, u32[]{:S(2)}, u32[]{:S(2)}) collective-permute-start(bf16[2,128]{1,0:T(2,128)(2,1)} %param.9), channel_id=1, source_target_pairs={{0,1},{1,0},{2,3},{3,2},{4,5},{5,4},{6,7},{7,6},{8,9},{9,8},{10,11... | collective-permute-start | bytes 1544 | tf_op jit(solution)/shard_map/ppermute | solution.py:113
  4.2 11.1 %copy-start.4 = (s32[1,1,16]{2,1,0:T(1,128)S(1)}, s32[1,1,16]{2,1,0:T(1,128)}, u32[]{:S(2)}) copy-start(s32[1,1,16]{2,1,0:T(1,128)} %param.15) | copy-start | bytes 196
  4.2 11.1 %copy-start.5 = (s32[1,1,16]{2,1,0:T(1,128)S(1)}, s32[1,1,16]{2,1,0:T(1,128)}, u32[]{:S(2)}) copy-start(s32[1,1,16]{2,1,0:T(1,128)} %param.14) | copy-start | bytes 196
  6.0 9.4 %copy-start = (f32[1,32,128]{2,1,0:T(8,128)S(1)}, f32[1,32,128]{2,1,0:T(8,128)}, u32[]{:S(2)}) copy-start(f32[1,32,128]{2,1,0:T(8,128)} %param.11) | copy-start | bytes 49156
  6.0 41.6 %copy-start.1 = (f32[1,32,128]{2,1,0:T(8,128)S(1)}, f32[1,32,128]{2,1,0:T(8,128)}, u32[]{:S(2)}) copy-start(f32[1,32,128]{2,1,0:T(8,128)} %param.10) | copy-start | bytes 49156
  6.0 73.0 %copy-start.3 = (bf16[2,128]{1,0:T(2,128)(2,1)S(1)}, bf16[2,128]{1,0:T(2,128)(2,1)}, u32[]{:S(2)}) copy-start(bf16[2,128]{1,0:T(2,128)(2,1)} %param.9) | copy-start | bytes 1540
  7.8 85.6 %copy-start.7 = (u32[32]{0:T(128)S(1)}, u32[32]{0:T(128)}, u32[]{:S(2)}) copy-start(u32[32]{0:T(128)} %constant.231) | copy-start | bytes 388
  79.1 4.1 %collective-permute-start.1 = (bf16[4,128]{1,0:T(4,128)(2,1)S(1)}, bf16[4,128]{1,0:T(4,128)(2,1)S(1)}, u32[]{:S(2)}, u32[]{:S(2)}) collective-permute-start(bf16[4,128]{1,0:T(4,128)(2,1)S(1)} %maximum_select_fusion.3), channel_id=1, source_target_pairs={{0,2},{1,3},{2,0},{3,1},{4,6},{5,7},{6,4},{7,5},{8,10},{9,11},{10,... | collective-permute-start | bytes 3080 | tf_op jit(solution)/shard_map/ppermute | solution.py:113
  83.2 3.7 %collective-permute-start.2 = (bf16[8,128]{1,0:T(8,128)(2,1)S(1)}, bf16[8,128]{1,0:T(8,128)(2,1)S(1)}, u32[]{:S(2)}, u32[]{:S(2)}) collective-permute-start(bf16[8,128]{1,0:T(8,128)(2,1)S(1)} %maximum_select_fusion.2), channel_id=1, source_target_pairs={{0,4},{1,5},{2,6},{3,7},{4,0},{5,1},{6,2},{7,3},{8,12},{9,13},{10,... | collective-permute-start | bytes 6152 | tf_op jit(solution)/shard_map/ppermute | solution.py:113
  87.0 4.6 %collective-permute-start.3 = (bf16[16,128]{1,0:T(8,128)(2,1)S(1)}, bf16[16,128]{1,0:T(8,128)(2,1)S(1)}, u32[]{:S(2)}, u32[]{:S(2)}) collective-permute-start(bf16[16,128]{1,0:T(8,128)(2,1)S(1)} %maximum_select_fusion.1), channel_id=1, source_target_pairs={{0,8},{1,9},{2,10},{3,11},{4,12},{5,13},{6,14},{7,15},{8,0},{9,1},... | collective-permute-start | bytes 12296 | tf_op jit(solution)/shard_map/ppermute | solution.py:113
  91.7 3.0 %collective-permute-start.4 = (bf16[32,15]{1,0:T(8,128)(2,1)S(1)}, bf16[32,15]{1,0:T(8,128)(2,1)S(1)}, u32[]{:S(2)}, u32[]{:S(2)}) collective-permute-start(bf16[32,15]{1,0:T(8,128)(2,1)S(1)} %get-tuple-element.389), channel_id=1, source_target_pairs={} | collective-permute-start | bytes 2888 | tf_op jit(solution)/shard_map/ppermute | solution.py:18
  92.3 2.4 %collective-permute-start.5 = (bf16[32,15]{1,0:T(8,128)(2,1)S(1)}, bf16[32,15]{1,0:T(8,128)(2,1)S(1)}, u32[]{:S(2)}, u32[]{:S(2)}) collective-permute-start(bf16[32,15]{1,0:T(8,128)(2,1)S(1)} %get-tuple-element.390), channel_id=1, source_target_pairs={} | collective-permute-start | bytes 2888 | tf_op jit(solution)/shard_map/ppermute | solution.py:20
  94.7 4.8 %copy-start.8 = (bf16[7,158,128]{1,0,2:T(8,128)(2,1)S(1)}, bf16[7,158,128]{1,0,2:T(8,128)(2,1)}, u32[]{:S(2)}) copy-start(bf16[7,158,128]{1,0,2:T(8,128)(2,1)} %fusion.28) | copy-start | bytes 849412
  166.6 60.8 %copy-start.2 = (f32[50]{0:T(128)}, f32[50]{0:T(128)S(1)}, u32[]{:S(2)}) copy-start(f32[50]{0:T(128)S(1)} %get-tuple-element.611) | copy-start | bytes 604
